TPU v7x, 128 devices: a whole 4x4x4 slice. The times are simulated.
128 devices in a mesh: section: 2 (over core), dp: 4 (over x), mp: 16 (over z, y).
Axes of the slice: x: 4, y: 4, z: 4, core: 2. Of those that a mesh axis runs over, the one named last changes fastest.
Arguments:
- segment_input: bfloat16 [2, 4, 256, 2048], P(None, 'dp', None, 'mp'), may hold values from -6 to 6
- out_grad: bfloat16 [2, 4, 256, 2048], P(None, 'dp', None, 'mp'), may hold values from -6 to 6
- pool_tokens: bfloat16 [16, 4, 128, 896], P('section', 'dp'), may hold values from -6 to 6
- neighbour_ids: int32 [2, 4, 4, 4], P(None, 'dp'), may hold values from 0 to 15, as said below
- neighbour_counts: int32 [2, 4, 4], P(None, 'dp'), may hold values from 1 to 4
- enc_gain: float32 [896], replicated, may hold values from 0.5 to 1.5
- enc_up: bfloat16 [896, 4096], P(None, 'mp'), may hold values from -0.1875 to 0.1875
- enc_down: bfloat16 [4096, 896], P(None, 'mp'), may hold values from -0.09375 to 0.09375
- norm_gain: float32 [2, 2048], P('section'), may hold values from 0.5 to 1.5
- w_query: bfloat16 [2, 2048, 4096], P('section', None, 'mp'), may hold values from -0.125 to 0.125
- w_key: bfloat16 [2, 896, 4096], P('section', None, 'mp'), may hold values from -0.1875 to 0.1875
- w_value: bfloat16 [2, 896, 4096], P('section', None, 'mp'), may hold values from -0.1875 to 0.1875
- w_out: bfloat16 [2, 4096, 2048], P('section', None, 'mp'), may hold values from -0.09375 to 0.09375
Outputs:
- grad_key: bfloat16 [2, 896, 4096], P('section', None, 'mp')
- grad_value: bfloat16 [2, 896, 4096], P('section', None, 'mp')
Inputs may be any that keep to these rules, and one draw needn't show every extreme that they name: `neighbour_ids`: the 4 slots of one stretch name distinct pool stretches.
All inputs are finite; a program needn't handle non-finite values.
Results may differ from a plain program's by a relative error of at most 0.025.
Values may be sent and summed in bfloat16 or wider, within the bound.
A program may use at most 128 MiB of HBM per device.

v0:
```python
import jax
import jax.numpy as jnp
from jax import lax
from jax.sharding import PartitionSpec as P

HEAD = 128
NT = 128
EPSILON = 1e-05


def passed_along(value, axis, by):
    peers = lax.axis_size(axis)
    pairs = [(i, i + by) for i in range(peers) if 0 <= i + by < peers]
    return lax.ppermute(value, axis, pairs)


def rms_scale(values):
    return lax.rsqrt(jnp.mean(values * values, axis=-1, keepdims=True) + EPSILON)


def collect(tensor):
    return lax.all_gather(tensor, "mp", axis=1, tiled=True)


def collect_pair(first, second):
    return (
        lax.all_gather(first, "mp", axis=1, tiled=True),
        lax.all_gather(second, "mp", axis=1, tiled=True),
    )


def pass_on(tensor, offset):
    return passed_along(tensor, "section", offset)


def attend(queries, key_block, value_block, usable):
    scores = jnp.einsum("cqhe,ckhe->chqk", queries, key_block, preferred_element_type=jnp.float32)
    scores = jnp.where(usable[:, None, None, :], scores, -1e30)
    weights = jax.nn.softmax(scores, axis=-1)
    weights_bf = weights.astype(jnp.bfloat16)
    attended = jnp.einsum(
        "chqk,ckhe->cqhe", weights_bf, value_block, preferred_element_type=jnp.float32
    )
    return (weights, weights_bf, attended.astype(jnp.bfloat16))


def attend_back(queries, key_block, value_block, weights, weights_bf, grad_attended):
    grad_weights = jnp.einsum(
        "cqhe,ckhe->chqk", grad_attended, value_block, preferred_element_type=jnp.float32
    )
    grad_scores = weights * (grad_weights - jnp.sum(weights * grad_weights, axis=-1, keepdims=True))
    grad_values = jnp.einsum(
        "chqk,cqhe->ckhe", weights_bf, grad_attended, preferred_element_type=jnp.float32
    ).astype(jnp.bfloat16)
    grad_keys = jnp.einsum("chqk,cqhe->ckhe", grad_scores, queries.astype(jnp.float32)).astype(
        jnp.bfloat16
    )
    grad_queries = jnp.einsum("chqk,ckhe->cqhe", grad_scores, key_block.astype(jnp.float32))
    return (grad_keys, grad_values, grad_queries)


def front(rows_in, gain_full, query_cols, key_block, value_block, usable, head_count):
    rows_wide = rows_in.astype(jnp.float32)
    inv_rms = rms_scale(rows_wide)
    normed = (rows_wide * inv_rms * gain_full).astype(jnp.bfloat16)
    query_raw = jnp.dot(normed, query_cols, preferred_element_type=jnp.float32)
    queries = (query_raw * HEAD ** (-0.5)).astype(jnp.bfloat16)
    queries = queries.reshape(key_block.shape[0], -1, head_count, HEAD)
    weights, weights_bf, attended = attend(queries, key_block, value_block, usable)
    return (inv_rms, query_raw, queries, weights, weights_bf, attended)


def on_device(
    segment_input,
    out_grad,
    pool_tokens,
    neighbour_ids,
    neighbour_counts,
    enc_gain,
    enc_up,
    enc_down,
    norm_gain,
    w_query,
    w_key,
    w_value,
    w_out,
):
    model_count = lax.axis_size("mp")
    model_index = lax.axis_index("mp")
    segment_count = lax.axis_size("section")
    segment_index = lax.axis_index("section")
    micro_count = segment_input.shape[0]
    row_count = segment_input.shape[2]
    feat_count = segment_input.shape[3]
    width = feat_count * model_count
    head_count = w_query.shape[2] // HEAD
    tract_count = neighbour_ids.shape[2]
    key_span = neighbour_ids.shape[3] * NT
    raw_rows = pool_tokens[:, 0].reshape(-1, pool_tokens.shape[3])
    raw_wide = raw_rows.astype(jnp.float32)
    enc_normed = (raw_wide * rms_scale(raw_wide) * enc_gain).astype(jnp.bfloat16)
    hidden_part = jax.nn.gelu(
        jnp.dot(enc_normed, enc_up, preferred_element_type=jnp.float32)
    ).astype(jnp.bfloat16)
    hidden_full = collect(hidden_part)
    enc_feat = enc_down.shape[1]
    raw_slice = lax.dynamic_slice_in_dim(raw_wide, model_index * enc_feat, enc_feat, 1)
    encoded = (
        raw_slice + jnp.dot(hidden_full, enc_down, preferred_element_type=jnp.float32)
    ).astype(jnp.bfloat16)
    slot_ids = neighbour_ids[:, 0].reshape(-1)
    shard_rows = encoded.shape[0]
    token_index = jnp.arange(NT, dtype=jnp.int32)
    global_rows = ((slot_ids * NT)[:, None] + token_index[None, :]).reshape(-1)
    empty_pool = jnp.zeros((segment_count * shard_rows, enc_feat * model_count), jnp.bfloat16)
    portion = lax.all_gather(encoded, ("section", "mp"), axis=0, tiled=True)
    shard_total = portion.shape[0] // shard_rows

    def one_shard(position, whole_pool):
        shard_block = lax.dynamic_slice_in_dim(portion, position * shard_rows, shard_rows, 0)
        row_start = position // model_count * shard_rows
        col_start = position % model_count * enc_feat
        return lax.dynamic_update_slice(whole_pool, shard_block, (row_start, col_start))

    whole_pool = lax.fori_loop(0, shard_total, one_shard, empty_pool)
    neighbours = jnp.take(whole_pool, global_rows, axis=0)

    def project(weight):
        projected = jnp.dot(neighbours, weight[0], preferred_element_type=jnp.float32).astype(
            jnp.bfloat16
        )
        return projected.reshape(micro_count, tract_count, key_span, head_count, HEAD)

    key_all = project(w_key)
    value_all = project(w_value)
    span_index = jnp.arange(key_span, dtype=jnp.int32) // NT
    usable_all = span_index[None, None, :] < neighbour_counts[:, 0][:, :, None]
    query_cols = w_query[0]
    out_cols = w_out[0]
    query_rows, out_rows = (
        lax.all_to_all(query_cols, "mp", split_axis=0, concat_axis=1, tiled=True),
        lax.all_to_all(out_cols, "mp", split_axis=0, concat_axis=1, tiled=True),
    )
    gain_full = norm_gain[0]
    gain_own = lax.dynamic_slice_in_dim(gain_full, model_index * feat_count, feat_count, 0)
    inputs_own = segment_input[:, 0]
    grads_own = out_grad[:, 0]
    step_count = micro_count + segment_count - 1
    empty_share = jnp.zeros((row_count, feat_count), jnp.bfloat16)
    stored_start = jnp.zeros((micro_count, row_count, width), jnp.bfloat16)

    def forward_step(step, state):
        received, stored = state
        which = step - segment_index
        active = (which >= 0) & (which < micro_count)
        which = jnp.clip(which, 0, micro_count - 1)
        incoming = jnp.where(segment_index == 0, inputs_own[which], received)
        rows_full = collect(incoming)
        outputs = front(
            rows_full,
            gain_full,
            query_cols,
            key_all[which],
            value_all[which],
            usable_all[which],
            head_count,
        )
        attended = collect(outputs[5].reshape(row_count, -1))
        result = incoming.astype(jnp.float32) + jnp.dot(
            attended, out_cols, preferred_element_type=jnp.float32
        )
        stored = stored.at[which].set(jnp.where(active, rows_full, stored[which]))
        return (pass_on(result.astype(jnp.bfloat16), 1), stored)

    _, stored = lax.fori_loop(0, step_count, forward_step, (empty_share, stored_start))
    grad_start = jnp.zeros((micro_count, tract_count, key_span, head_count, HEAD), jnp.bfloat16)

    def backward_step(step, state):
        received, key_grads, value_grads = state
        which = step - (segment_count - 1 - segment_index)
        active = (which >= 0) & (which < micro_count)
        which = jnp.clip(which, 0, micro_count - 1)
        incoming = jnp.where(segment_index == segment_count - 1, grads_own[which], received)
        rows_full = stored[which]
        rows_own = lax.dynamic_slice_in_dim(rows_full, model_index * feat_count, feat_count, 1)
        key_block = key_all[which]
        value_block = value_all[which]
        inv_rms, query_raw, queries, weights, weights_bf, _ = front(
            rows_full, gain_full, query_cols, key_block, value_block, usable_all[which], head_count
        )
        grad_full = collect(incoming)
        grad_att = jnp.dot(grad_full, out_rows.T, preferred_element_type=jnp.float32).astype(
            jnp.bfloat16
        )
        grad_att = grad_att.reshape(queries.shape)
        grad_keys, grad_values, grad_queries = attend_back(
            queries, key_block, value_block, weights, weights_bf, grad_att
        )
        grad_scaled = (grad_queries * HEAD ** (-0.5)).reshape(row_count, -1).astype(jnp.bfloat16)
        part_total = jnp.sum(
            grad_scaled.astype(jnp.float32) * query_raw, axis=1, keepdims=True
        ).astype(jnp.bfloat16)
        scaled_full, totals = collect_pair(grad_scaled, part_total)
        row_total = jnp.sum(totals.astype(jnp.float32), axis=1, keepdims=True)
        grad_normed = jnp.dot(scaled_full, query_rows.T, preferred_element_type=jnp.float32)
        rows_wide = rows_own.astype(jnp.float32)
        grad_in = (
            incoming.astype(jnp.float32)
            + inv_rms * gain_own * grad_normed
            - rows_wide * inv_rms * inv_rms * row_total / width
        )
        key_grads = key_grads.at[which].set(jnp.where(active, grad_keys, key_grads[which]))
        value_grads = value_grads.at[which].set(jnp.where(active, grad_values, value_grads[which]))
        return (pass_on(grad_in.astype(jnp.bfloat16), -1), key_grads, value_grads)

    _, key_grads, value_grads = lax.fori_loop(
        0, step_count, backward_step, (empty_share, grad_start, grad_start)
    )
    contract = (((0,), (0,)), ((), ()))
    key_sum = lax.dot_general(
        neighbours,
        key_grads.reshape(-1, head_count * HEAD),
        contract,
        preferred_element_type=jnp.float32,
    )
    value_sum = lax.dot_general(
        neighbours,
        value_grads.reshape(-1, head_count * HEAD),
        contract,
        preferred_element_type=jnp.float32,
    )
    key_total, value_total = (
        lax.psum(key_sum.astype(jnp.bfloat16), "dp").astype(jnp.float32),
        lax.psum(value_sum.astype(jnp.bfloat16), "dp").astype(jnp.float32),
    )
    return (key_total.astype(jnp.bfloat16)[None], value_total.astype(jnp.bfloat16)[None])


def solution(mesh):
    placed = (
        P(None, "dp", None, "mp"),
        P(None, "dp", None, "mp"),
        P("section", "dp", None, None),
        P(None, "dp", None, None),
        P(None, "dp", None),
        P(),
        P(None, "mp"),
        P(None, "mp"),
        P("section", None),
        P("section", None, "mp"),
        P("section", None, "mp"),
        P("section", None, "mp"),
        P("section", None, "mp"),
    )
    return jax.shard_map(
        on_device,
        mesh=mesh,
        in_specs=placed,
        out_specs=(P("section", None, "mp"), P("section", None, "mp")),
        check_vma=False,
    )
```

profile of v0, /device:TPU:0, one launch (start us, length us, event | category | flops | bytes accessed | tf_op | source)
XLA Modules:
  0.0 1101.6 jit_solution(5113289207940649873)
XLA Ops:
  12.3 4.0 fusion.112
  16.3 80.0 %all-gather.10.cloned.1.call-done = bf16[1024,4096]{1,0:T(8,128)(2,1)} async-done(((bf16[1024,256]{1,0:T(8,128)(2,1)}), bf16[1024,4096]{1,0:T(8,128)(2,1)}) %all-gather.10.cloned.1.call-update) | async-done | bytes 8388624 | tf_op jit(solution)/shard_map/all_gather | solution.py:22
  96.3 6.7 fusion.104
  103.0 5.1 all-to-all-start
  108.5 17.1 %all-to-all-done = bf16[16,256,128]{2,1,0:T(8,128)(2,1)S(1)} async-done(((bf16[16,256,128]{2,1,0:T(8,128)(2,1)}), bf16[16,256,128]{2,1,0:T(8,128)(2,1)S(1)}, u32[]{:S(2)}, u32[]{:S(2)}) %all-to-all-start) | async-done | bytes 1048608 | tf_op jit(solution)/shard_map/all_to_all | solution.py:142
  125.6 3.8 all-to-all-start.1
  133.1 13.0 %all-to-all-done.1 = bf16[16,128,256]{2,1,0:T(8,128)(2,1)S(1)} async-done(((bf16[16,128,256]{2,1,0:T(8,128)(2,1)}), bf16[16,128,256]{2,1,0:T(8,128)(2,1)S(1)}, u32[]{:S(2)}, u32[]{:S(2)}) %all-to-all-start.1) | async-done | bytes 1048608 | tf_op jit(solution)/shard_map/all_to_all | solution.py:141
  148.1 6.3 all-gather.12.cloned.1.call-done
  156.6 184.6 %while.54 = (s32[]{:T(128)}, bf16[2048,896]{1,0:T(8,128)(2,1)}, bf16[32768,56]{0,1:T(8,128)(2,1)}, s32[]{:T(128)}, s32[]{:T(128)}, /*index=5*/s32[]{:T(128)}, s3...) while((s32[]{:T(128)}, bf16[2048,896]{1,0:T(8,128)(2,1)}, ...), condition=%wide.region_2.3_spmd, body=%wide.region_1.2_spmd.sunk | while | flops 26 | bytes 688530 | solution.py:125
  157.7 4.6 dynamic_update_slice.11
  163.4 5.2 dynamic_update_slice.11
  169.7 5.2 dynamic_update_slice.11
  176.0 5.2 dynamic_update_slice.11
  182.3 5.2 dynamic_update_slice.11
  188.6 5.3 dynamic_update_slice.11
  195.0 5.3 dynamic_update_slice.11
  201.3 5.2 dynamic_update_slice.11
  207.7 5.2 dynamic_update_slice.11
  214.0 5.2 dynamic_update_slice.11
  220.3 5.2 dynamic_update_slice.11
  226.6 5.2 dynamic_update_slice.11
  232.9 5.2 dynamic_update_slice.11
  239.2 5.2 dynamic_update_slice.11
  245.5 4.6 dynamic_update_slice.11
  251.2 4.6 dynamic_update_slice.11
  256.9 3.7 dynamic_update_slice.11
  261.6 4.3 dynamic_update_slice.11
  267.1 4.3 dynamic_update_slice.11
  272.5 4.3 dynamic_update_slice.11
  277.9 4.3 dynamic_update_slice.11
  283.3 4.3 dynamic_update_slice.11
  288.8 4.3 dynamic_update_slice.11
  294.2 4.3 dynamic_update_slice.11
  299.6 4.3 dynamic_update_slice.11
  305.0 4.3 dynamic_update_slice.11
  310.4 4.3 dynamic_update_slice.11
  315.8 4.3 dynamic_update_slice.11
  321.2 4.3 dynamic_update_slice.11
  326.6 4.3 dynamic_update_slice.11
  332.0 4.0 dynamic_update_slice.11
  337.2 4.0 dynamic_update_slice.11
  341.2 22.4 %gather_fusion = bf16[4096,896]{1,0:T(8,128)(2,1)} fusion(bf16[2048,896]{1,0:T(8,128)(2,1)} %get-tuple-element.835, s32[4096]{0:T(1024)S(1)} %broadcast_clamp_fusion), kind=kCustom, calls=%fused_computation | custom fusion | bytes 14696448 | tf_op jit(solution)/shard_map/jit(_take)/gather | solution.py:126
  363.6 5.8 convolution_convert_fusion.4
  373.8 5.7 convolution_convert_fusion.5
  385.3 318.6 %while.55 = (s32[]{:T(128)}, bf16[256,128]{1,0:T(8,128)(2,1)S(1)}, bf16[2,256,2048]{2,1,0:T(8,128)(2,1)}, pred[]{:T(512)}, s32[]{:T(128)}, /*index=5*/bf16[2,256...) while((s32[]{:T(128)}, bf16[256,128]{1,0:T(8,128)(2,1)S(1)}, ...), condition=%wide.region_8.9_spmd, body=%wide.region_3.8_spmd.sunk | while | flops 677446400 | bytes 32006564 | solution.py:175
  386.1 45.0 %all-gather.14.cloned.1.call-done = bf16[256,2048]{1,0:T(8,128)(2,1)} async-done(((bf16[256,128]{1,0:T(8,128)(2,1)}), bf16[256,2048]{1,0:T(8,128)(2,1)}) %all-gather.14.cloned.1.call-update) | async-done | bytes 1048592 | tf_op jit(solution)/shard_map/while/body/eval_jaxpr/all_gather | solution.py:22
  441.1 44.5 %all-gather.16.cloned.1.call-done = bf16[256,4096]{1,0:T(8,128)(2,1)} async-done(((bf16[256,256]{1,0:T(8,128)(2,1)}), bf16[256,4096]{1,0:T(8,128)(2,1)}) %all-gather.16.cloned.1.call-update) | async-done | bytes 2097168 | tf_op jit(solution)/shard_map/while/body/eval_jaxpr/all_gather | solution.py:22
  492.2 45.0 %all-gather.14.cloned.1.call-done = bf16[256,2048]{1,0:T(8,128)(2,1)} async-done(((bf16[256,128]{1,0:T(8,128)(2,1)}), bf16[256,2048]{1,0:T(8,128)(2,1)}) %all-gather.14.cloned.1.call-update) | async-done | bytes 1048592 | tf_op jit(solution)/shard_map/while/body/eval_jaxpr/all_gather | solution.py:22
  547.2 44.5 %all-gather.16.cloned.1.call-done = bf16[256,4096]{1,0:T(8,128)(2,1)} async-done(((bf16[256,256]{1,0:T(8,128)(2,1)}), bf16[256,4096]{1,0:T(8,128)(2,1)}) %all-gather.16.cloned.1.call-update) | async-done | bytes 2097168 | tf_op jit(solution)/shard_map/while/body/eval_jaxpr/all_gather | solution.py:22
  598.3 45.2 %all-gather.14.cloned.1.call-done = bf16[256,2048]{1,0:T(8,128)(2,1)} async-done(((bf16[256,128]{1,0:T(8,128)(2,1)}), bf16[256,2048]{1,0:T(8,128)(2,1)}) %all-gather.14.cloned.1.call-update) | async-done | bytes 1048592 | tf_op jit(solution)/shard_map/while/body/eval_jaxpr/all_gather | solution.py:22
  653.6 44.5 %all-gather.16.cloned.1.call-done = bf16[256,4096]{1,0:T(8,128)(2,1)} async-done(((bf16[256,256]{1,0:T(8,128)(2,1)}), bf16[256,4096]{1,0:T(8,128)(2,1)}) %all-gather.16.cloned.1.call-update) | async-done | bytes 2097168 | tf_op jit(solution)/shard_map/while/body/eval_jaxpr/all_gather | solution.py:22
  708.8 323.1 %while.56 = (s32[]{:T(128)}, bf16[256,128]{1,0:T(8,128)(2,1)S(1)}, bf16[2,4,512,2,128]{4,3,2,1,0:T(2,128)(2,1)}, bf16[2,4,512,2,128]{4,3,2,1,0:T(2,128)(2,1)}, p...) while((s32[]{:T(128)}, bf16[256,128]{1,0:T(8,128)(2,1)S(1)}, ...), condition=%wide.region_17.18_spmd, body=%wide.region_9.17_spmd.sunk | while | flops 1152261888 | bytes 76540544 | solution.py:216
  715.5 39.3 %all-gather.18.cloned.1.call-done = bf16[256,2048]{1,0:T(8,128)(2,1)} async-done(((bf16[256,128]{1,0:T(8,128)(2,1)}), bf16[256,2048]{1,0:T(8,128)(2,1)}) %all-gather.18.cloned.1.call-update) | async-done | bytes 1048592 | tf_op jit(solution)/shard_map/while/body/eval_jaxpr/all_gather | solution.py:22
  776.4 3.8 fusion.198
  782.7 22.8 %all-gather.2 = bf16[16,1,256]{2,1,0:T(2,128)(2,1)S(1)} all-gather(bf16[1,1,256]{2,1,0:T(2,128)(2,1)S(1)} %reshape.462), channel_id=1, replica_groups=mesh['section'=2,'dp'=4,'mp'=16] {'mp'}, dimensions={0}, use_global_device_ids=true | all-gather | bytes 8704 | tf_op jit(solution)/shard_map/while/body/eval_jaxpr/all_gather | solution.py:28
  822.7 40.1 %all-gather.18.cloned.1.call-done = bf16[256,2048]{1,0:T(8,128)(2,1)} async-done(((bf16[256,128]{1,0:T(8,128)(2,1)}), bf16[256,2048]{1,0:T(8,128)(2,1)}) %all-gather.18.cloned.1.call-update) | async-done | bytes 1048592 | tf_op jit(solution)/shard_map/while/body/eval_jaxpr/all_gather | solution.py:22
  884.3 3.8 fusion.198
  890.7 22.8 %all-gather.2 = bf16[16,1,256]{2,1,0:T(2,128)(2,1)S(1)} all-gather(bf16[1,1,256]{2,1,0:T(2,128)(2,1)S(1)} %reshape.462), channel_id=1, replica_groups=mesh['section'=2,'dp'=4,'mp'=16] {'mp'}, dimensions={0}, use_global_device_ids=true | all-gather | bytes 8704 | tf_op jit(solution)/shard_map/while/body/eval_jaxpr/all_gather | solution.py:28
  930.7 40.1 %all-gather.18.cloned.1.call-done = bf16[256,2048]{1,0:T(8,128)(2,1)} async-done(((bf16[256,128]{1,0:T(8,128)(2,1)}), bf16[256,2048]{1,0:T(8,128)(2,1)}) %all-gather.18.cloned.1.call-update) | async-done | bytes 1048592 | tf_op jit(solution)/shard_map/while/body/eval_jaxpr/all_gather | solution.py:22
  992.3 3.8 fusion.198
  998.7 22.8 %all-gather.2 = bf16[16,1,256]{2,1,0:T(2,128)(2,1)S(1)} all-gather(bf16[1,1,256]{2,1,0:T(2,128)(2,1)S(1)} %reshape.462), channel_id=1, replica_groups=mesh['section'=2,'dp'=4,'mp'=16] {'mp'}, dimensions={0}, use_global_device_ids=true | all-gather | bytes 8704 | tf_op jit(solution)/shard_map/while/body/eval_jaxpr/all_gather | solution.py:28
  1031.9 7.4 fusion.101
  1039.3 6.7 fusion.98
  1046.1 45.3 %all-reduce.3.cloned.1.call-done = (bf16[1,896,256]{2,1,0:T(8,128)(2,1)}, bf16[1,896,256]{2,1,0:T(8,128)(2,1)}) async-done(((bf16[1,896,256]{2,1,0:T(8,128)(2,1)}, bf16[1,896,256]{2,1,0:T(8,128)(2,1)}), (bf16[1,896,256]{2,1,0:T(8,128)(2,1)}, bf16[1,896,256]{2,1,0:T(8,128)(2,1)})) %all-reduce.3.cloned.1.call-update) | async-done | bytes 917520 | tf_op jit(solution)/shard_map/psum | solution.py:233
  (338 shorter events, 239.3 us)
Async XLA Ops:
  7.2 356.4 %copy-start = (bf16[1,896,256]{2,1,0:T(8,128)(2,1)S(1)}, bf16[1,896,256]{2,1,0:T(8,128)(2,1)}, u32[]{:S(2)}) copy-start(bf16[1,896,256]{2,1,0:T(8,128)(2,1)} %param.35) | copy-start | bytes 1376260
  7.2 2.1 copy-start.9
  7.2 89.1 %all-gather.10.cloned.1.call-start = ((), (), s32[]{:S(2)}) async-start(), calls=%async_computation.2 | async-start | bytes 8912896 | tf_op jit(solution)/shard_map/all_gather | solution.py:22
  9.3 2.9 copy-start.16
  9.3 2.9 copy-start.19
  12.3 84.0 %copy-start.12 = (bf16[4096,56]{0,1:T(8,128)(2,1)S(1)}, bf16[4096,56]{0,1:T(8,128)(2,1)}, u32[]{:S(2)}) copy-start(bf16[4096,56]{0,1:T(8,128)(2,1)} %param.32) | copy-start | bytes 1376260
  16.3 138.2 %all-gather.12.cloned.1.call-start = ((), (), s32[]{:S(2)}) async-start(), calls=%async_computation.3 | async-start | bytes 3784704 | tf_op jit(solution)/shard_map/all_gather | solution.py:116
  103.0 5.1 copy-start.14
  103.0 5.2 copy-start.18
  103.0 5.3 copy-start.15
  103.0 22.6 %all-to-all-start = ((bf16[16,256,128]{2,1,0:T(8,128)(2,1)}), bf16[16,256,128]{2,1,0:T(8,128)(2,1)S(1)}, u32[]{:S(2)}, u32[]{:S(2)}) async-start(bf16[16,256,128]{2,1,0:T(8,128)(2,1)} %bitcast.38), calls=%async_computation | async-start | bytes 2097152 | tf_op jit(solution)/shard_map/all_to_all | solution.py:142
  125.6 20.5 %all-to-all-start.1 = ((bf16[16,128,256]{2,1,0:T(8,128)(2,1)}), bf16[16,128,256]{2,1,0:T(8,128)(2,1)S(1)}, u32[]{:S(2)}, u32[]{:S(2)}) async-start(bf16[16,128,256]{2,1,0:T(8,128)(2,1)} %bitcast.41), calls=%async_computation.1 | async-start | bytes 2097152 | tf_op jit(solution)/shard_map/all_to_all | solution.py:141
  371.9 1.8 copy-start.17
  383.7 1.6 copy-start.10
  383.7 1.6 copy-start.13
  385.3 45.8 %all-gather.14.cloned.1.call-start = ((), (), s32[]{:S(2)}) async-start(), calls=%async_computation.5 | async-start | bytes 1114112 | tf_op jit(solution)/shard_map/while/body/eval_jaxpr/all_gather | solution.py:22
  386.0 99.5 %all-gather.16.cloned.1.call-start = ((), (), s32[]{:S(2)}) async-start(), calls=%async_computation.6 | async-start | bytes 2228224 | tf_op jit(solution)/shard_map/while/body/eval_jaxpr/all_gather | solution.py:22
  438.2 47.4 %copy-start.8 = (bf16[256,128]{1,0:T(8,128)(2,1)S(1)}, bf16[256,128]{1,0:T(8,128)(2,1)}, u32[]{:S(2)}) copy-start(bf16[256,128]{1,0:T(8,128)(2,1)} %bitcast_select_fusion.6) | copy-start | bytes 196612 | tf_op jit(solution)/shard_map/while
  441.1 48.3 %copy-start.2 = (bf16[256,2048]{1,0:T(8,128)(2,1)S(1)}, bf16[256,2048]{1,0:T(8,128)(2,1)}, u32[]{:S(2)}) copy-start(bf16[256,2048]{1,0:T(8,128)(2,1)} %all-gather.14.cloned.1.call-done) | copy-start | bytes 3145732 | tf_op jit(solution)/shard_map/while
  488.2 3.3 collective-permute-start
  491.5 45.7 %all-gather.14.cloned.1.call-start = ((), (), s32[]{:S(2)}) async-start(), calls=%async_computation.5 | async-start | bytes 1114112 | tf_op jit(solution)/shard_map/while/body/eval_jaxpr/all_gather | solution.py:22
  492.1 99.6 %all-gather.16.cloned.1.call-start = ((), (), s32[]{:S(2)}) async-start(), calls=%async_computation.6 | async-start | bytes 2228224 | tf_op jit(solution)/shard_map/while/body/eval_jaxpr/all_gather | solution.py:22
  544.3 47.4 %copy-start.8 = (bf16[256,128]{1,0:T(8,128)(2,1)S(1)}, bf16[256,128]{1,0:T(8,128)(2,1)}, u32[]{:S(2)}) copy-start(bf16[256,128]{1,0:T(8,128)(2,1)} %bitcast_select_fusion.6) | copy-start | bytes 196612 | tf_op jit(solution)/shard_map/while
  547.2 48.3 %copy-start.2 = (bf16[256,2048]{1,0:T(8,128)(2,1)S(1)}, bf16[256,2048]{1,0:T(8,128)(2,1)}, u32[]{:S(2)}) copy-start(bf16[256,2048]{1,0:T(8,128)(2,1)} %all-gather.14.cloned.1.call-done) | copy-start | bytes 3145732 | tf_op jit(solution)/shard_map/while
  594.2 3.3 collective-permute-start
  597.5 46.0 %all-gather.14.cloned.1.call-start = ((), (), s32[]{:S(2)}) async-start(), calls=%async_computation.5 | async-start | bytes 1114112 | tf_op jit(solution)/shard_map/while/body/eval_jaxpr/all_gather | solution.py:22
  598.3 99.8 %all-gather.16.cloned.1.call-start = ((), (), s32[]{:S(2)}) async-start(), calls=%async_computation.6 | async-start | bytes 2228224 | tf_op jit(solution)/shard_map/while/body/eval_jaxpr/all_gather | solution.py:22
  650.7 47.4 %copy-start.8 = (bf16[256,128]{1,0:T(8,128)(2,1)S(1)}, bf16[256,128]{1,0:T(8,128)(2,1)}, u32[]{:S(2)}) copy-start(bf16[256,128]{1,0:T(8,128)(2,1)} %bitcast_select_fusion.6) | copy-start | bytes 196612 | tf_op jit(solution)/shard_map/while
  653.6 48.3 %copy-start.2 = (bf16[256,2048]{1,0:T(8,128)(2,1)S(1)}, bf16[256,2048]{1,0:T(8,128)(2,1)}, u32[]{:S(2)}) copy-start(bf16[256,2048]{1,0:T(8,128)(2,1)} %all-gather.14.cloned.1.call-done) | copy-start | bytes 3145732 | tf_op jit(solution)/shard_map/while
  700.6 3.3 collective-permute-start
  703.9 4.8 copy-start.11
  704.0 4.8 copy-start.20
  708.8 46.0 %all-gather.18.cloned.1.call-start = ((), (), s32[]{:S(2)}) async-start(), calls=%async_computation.7 | async-start | bytes 1114112 | tf_op jit(solution)/shard_map/while/body/eval_jaxpr/all_gather | solution.py:22
  709.5 98.6 %all-gather.20.cloned.1.call-start = ((), (), s32[]{:S(2)}) async-start(), calls=%async_computation.8 | async-start | bytes 2228224 | tf_op jit(solution)/shard_map/while/body/eval_jaxpr/all_gather | solution.py:27
  758.7 2.0 copy-start.21
  765.5 4.8 copy-start.3
  780.2 27.9 %copy-start.7 = (bf16[256,128]{1,0:T(8,128)(2,1)S(1)}, bf16[256,128]{1,0:T(8,128)(2,1)}, u32[]{:S(2)}) copy-start(bf16[256,128]{1,0:T(8,128)(2,1)} %bitcast_select_fusion.7) | copy-start | bytes 196612 | tf_op jit(solution)/shard_map/while
  808.1 4.0 copy-start.4
  810.8 3.8 collective-permute-start.1
  814.6 1.3 copy-start.5
  815.9 46.8 %all-gather.18.cloned.1.call-start = ((), (), s32[]{:S(2)}) async-start(), calls=%async_computation.7 | async-start | bytes 1114112 | tf_op jit(solution)/shard_map/while/body/eval_jaxpr/all_gather | solution.py:22
  816.7 99.4 %all-gather.20.cloned.1.call-start = ((), (), s32[]{:S(2)}) async-start(), calls=%async_computation.8 | async-start | bytes 2228224 | tf_op jit(solution)/shard_map/while/body/eval_jaxpr/all_gather | solution.py:27
  866.6 2.0 copy-start.21
  873.5 4.8 copy-start.3
  888.1 27.9 %copy-start.7 = (bf16[256,128]{1,0:T(8,128)(2,1)S(1)}, bf16[256,128]{1,0:T(8,128)(2,1)}, u32[]{:S(2)}) copy-start(bf16[256,128]{1,0:T(8,128)(2,1)} %bitcast_select_fusion.7) | copy-start | bytes 196612 | tf_op jit(solution)/shard_map/while
  916.1 4.0 copy-start.4
  918.8 3.8 collective-permute-start.1
  922.6 1.3 copy-start.5
  923.9 46.8 %all-gather.18.cloned.1.call-start = ((), (), s32[]{:S(2)}) async-start(), calls=%async_computation.7 | async-start | bytes 1114112 | tf_op jit(solution)/shard_map/while/body/eval_jaxpr/all_gather | solution.py:22
  924.6 99.4 %all-gather.20.cloned.1.call-start = ((), (), s32[]{:S(2)}) async-start(), calls=%async_computation.8 | async-start | bytes 2228224 | tf_op jit(solution)/shard_map/while/body/eval_jaxpr/all_gather | solution.py:27
  974.6 2.0 copy-start.21
  981.5 4.8 copy-start.3
  996.1 27.9 %copy-start.7 = (bf16[256,128]{1,0:T(8,128)(2,1)S(1)}, bf16[256,128]{1,0:T(8,128)(2,1)}, u32[]{:S(2)}) copy-start(bf16[256,128]{1,0:T(8,128)(2,1)} %bitcast_select_fusion.7) | copy-start | bytes 196612 | tf_op jit(solution)/shard_map/while
  1024.0 4.0 copy-start.4
  1026.8 3.8 collective-permute-start.1
  1030.6 1.3 copy-start.5
  1031.9 59.5 %all-reduce.3.cloned.1.call-start = ((), (), s32[]{:S(2)}) async-start(), calls=%async_computation.4 | async-start | bytes 1835008 | tf_op jit(solution)/shard_map/psum | solution.py:233
  1031.9 7.4 copy-start.6
  1039.3 55.7 %copy-start.1 = (bf16[1,896,256]{2,1,0:T(8,128)(2,1)S(1)}, bf16[1,896,256]{2,1,0:T(8,128)(2,1)}, u32[]{:S(2)}) copy-start(bf16[1,896,256]{2,1,0:T(8,128)(2,1)} %param.35) | copy-start | bytes 1376260
Sparse Core Ops, SparseCore 0:
  16.4 79.8 all-gather.9
  103.2 51.2 all-gather.11
  388.8 42.2 all-gather.13
  439.2 46.3 all-gather.15
  494.6 42.4 all-gather.13
  545.2 46.3 all-gather.15
  601.0 42.5 all-gather.13
  651.6 46.3 all-gather.15
  712.3 42.5 all-gather.17
  761.7 46.3 all-gather.19
  819.4 43.2 all-gather.17
  869.6 46.3 all-gather.19
  927.4 43.3 all-gather.17
  977.6 46.3 all-gather.19
  1046.2 45.1 all-reduce.2
where the time goes:
time: 1110 us; the launch traced here: 1100 us
  waiting for transfers between devices  558 us (50%)
  local copies, waits for them, and re-layouts  296 us (27%)
  matrix products  120 us (11%)
  blocking collectives  68.5 us (6%)
  other arithmetic  26 us (2%)
  starting transfers between devices  17 us (2%)
  between operations  13.9 us (1%)
    all_gather x10, waiting for transfers between devices, collect(): return lax.all_gather(tensor, 'mp', axis=1, tiled=True)  468 us
    dynamic_update_slice x32, local copies, waits for them, and re-layouts, one_shard(): lax.dynamic_update_slice(whole_pool, shard_block, (row_start, col_start))  149 us
    all_gather x3, blocking collectives, collect_pair(): lax.all_gather(second, 'mp', axis=1, tiled=True)  68.5 us
    psum x1, waiting for transfers between devices, on_device(): lax.psum(key_sum.astype(jnp.bfloat16), 'dp').astype(jnp.float32)  45.3 us
    dynamic_slice x64, local copies, waits for them, and re-layouts, one_shard(): lax.dynamic_slice_in_dim(portion, position * shard_rows, shard_rows, 0)  34.4 us
    gather x1, local copies, waits for them, and re-layouts, on_device(): neighbours = jnp.take(whole_pool, global_rows, axis=0)  22.4 us
  transfers between devices with their start and end apart: 23, of which 17 were waited for; matrix products, arithmetic and copies ran while one was open for 10% of the time, Pallas kernels for 0%

commit v1 on v0

--- a/solution.py
+++ b/solution.py
@@ -230,7 +230,7 @@
         preferred_element_type=jnp.float32,
     )
     key_total, value_total = (
-        lax.psum(key_sum.astype(jnp.bfloat16), "dp").astype(jnp.float32),
+        jnp.sum(lax.all_gather(key_sum.astype(jnp.bfloat16), "dp"), axis=0).astype(jnp.float32),
         lax.psum(value_sum.astype(jnp.bfloat16), "dp").astype(jnp.float32),
     )
     return (key_total.astype(jnp.bfloat16)[None], value_total.astype(jnp.bfloat16)[None])

time: 1110 us -> 1130 us (1.018)
  waiting for transfers between devices: 558 us -> 578 us
    all_gather x0 -> x1, waiting for transfers between devices: none -> 21.9 us  [on_device(): lax.all_gather(key_sum.astype(jnp.bfloat16), 'dp')]
  transfers between devices with their start and end apart: 23 -> 24, of which waited for: 17 -> 18; matrix products, arithmetic and copies ran while one was open for 10% -> 10% of each run, Pallas kernels for 0% -> 0%
where the time goes in v1:
time: 1130 us; the launch traced here: 1120 us
  waiting for transfers between devices  578 us (51%)
  local copies, waits for them, and re-layouts  295 us (26%)
  matrix products  119 us (11%)
  blocking collectives  68.3 us (6%)
  other arithmetic  28.1 us (2%)
  starting transfers between devices  17.1 us (2%)
  between operations  14 us (1%)
    all_gather x10, waiting for transfers between devices, collect(): return lax.all_gather(tensor, 'mp', axis=1, tiled=True)  468 us
    dynamic_update_slice x32, local copies, waits for them, and re-layouts, one_shard(): lax.dynamic_update_slice(whole_pool, shard_block, (row_start, col_start))  149 us
    all_gather x3, blocking collectives, collect_pair(): lax.all_gather(second, 'mp', axis=1, tiled=True)  68.3 us
    psum x1, waiting for transfers between devices, on_device(): lax.psum(value_sum.astype(jnp.bfloat16), 'dp').astype(jnp.float32)  42 us
    dynamic_slice x64, local copies, waits for them, and re-layouts, one_shard(): lax.dynamic_slice_in_dim(portion, position * shard_rows, shard_rows, 0)  34.4 us
  transfers between devices with their start and end apart: 24, of which 18 were waited for; matrix products, arithmetic and copies ran while one was open for 10% of the time, Pallas kernels for 0%

profile of v1, /device:TPU:0, one launch (start us, length us, event | category | flops | bytes accessed | tf_op | source)
XLA Modules:
  0.0 1121.5 jit_solution(8041011149730678347)
XLA Ops:
  12.3 4.0 fusion.109
  16.3 80.0 %all-gather.12.cloned.1.call-done = bf16[1024,4096]{1,0:T(8,128)(2,1)} async-done(((bf16[1024,256]{1,0:T(8,128)(2,1)}), bf16[1024,4096]{1,0:T(8,128)(2,1)}) %all-gather.12.cloned.1.call-update) | async-done | bytes 8388624 | tf_op jit(solution)/shard_map/all_gather | solution.py:22
  96.3 6.7 fusion.101
  103.0 5.1 all-to-all-start
  108.5 17.1 %all-to-all-done = bf16[16,256,128]{2,1,0:T(8,128)(2,1)S(1)} async-done(((bf16[16,256,128]{2,1,0:T(8,128)(2,1)}), bf16[16,256,128]{2,1,0:T(8,128)(2,1)S(1)}, u32[]{:S(2)}, u32[]{:S(2)}) %all-to-all-start) | async-done | bytes 1048608 | tf_op jit(solution)/shard_map/all_to_all | solution.py:142
  125.6 3.8 all-to-all-start.1
  133.1 13.0 %all-to-all-done.1 = bf16[16,128,256]{2,1,0:T(8,128)(2,1)S(1)} async-done(((bf16[16,128,256]{2,1,0:T(8,128)(2,1)}), bf16[16,128,256]{2,1,0:T(8,128)(2,1)S(1)}, u32[]{:S(2)}, u32[]{:S(2)}) %all-to-all-start.1) | async-done | bytes 1048608 | tf_op jit(solution)/shard_map/all_to_all | solution.py:141
  148.1 6.3 all-gather.14.cloned.1.call-done
  156.6 185.1 %while.54 = (s32[]{:T(128)}, bf16[2048,896]{1,0:T(8,128)(2,1)}, bf16[32768,56]{0,1:T(8,128)(2,1)}, s32[]{:T(128)}, s32[]{:T(128)}, /*index=5*/s32[]{:T(128)}, s3...) while((s32[]{:T(128)}, bf16[2048,896]{1,0:T(8,128)(2,1)}, ...), condition=%wide.region_2.3_spmd, body=%wide.region_1.2_spmd.sunk | while | flops 26 | bytes 688530 | solution.py:125
  157.7 4.6 dynamic_update_slice.11
  163.4 5.2 dynamic_update_slice.11
  169.8 5.2 dynamic_update_slice.11
  176.1 5.3 dynamic_update_slice.11
  182.4 5.3 dynamic_update_slice.11
  188.8 5.2 dynamic_update_slice.11
  195.1 5.2 dynamic_update_slice.11
  201.5 5.2 dynamic_update_slice.11
  207.8 5.2 dynamic_update_slice.11
  214.1 5.2 dynamic_update_slice.11
  220.4 5.3 dynamic_update_slice.11
  226.8 5.3 dynamic_update_slice.11
  233.2 5.2 dynamic_update_slice.11
  239.5 5.2 dynamic_update_slice.11
  245.9 4.6 dynamic_update_slice.11
  251.6 4.6 dynamic_update_slice.11
  262.0 4.3 dynamic_update_slice.11
  267.5 4.3 dynamic_update_slice.11
  272.9 4.3 dynamic_update_slice.11
  278.3 4.3 dynamic_update_slice.11
  283.7 4.3 dynamic_update_slice.11
  289.2 4.3 dynamic_update_slice.11
  294.6 4.3 dynamic_update_slice.11
  300.0 4.3 dynamic_update_slice.11
  305.4 4.3 dynamic_update_slice.11
  310.9 4.3 dynamic_update_slice.11
  316.3 4.3 dynamic_update_slice.11
  321.7 4.3 dynamic_update_slice.11
  327.1 4.3 dynamic_update_slice.11
  332.6 4.0 dynamic_update_slice.11
  337.7 4.0 dynamic_update_slice.11
  341.7 22.4 %gather_fusion = bf16[4096,896]{1,0:T(8,128)(2,1)} fusion(bf16[2048,896]{1,0:T(8,128)(2,1)} %get-tuple-element.835, s32[4096]{0:T(1024)S(1)} %broadcast_clamp_fusion), kind=kCustom, calls=%fused_computation | custom fusion | bytes 14696448 | tf_op jit(solution)/shard_map/jit(_take)/gather | solution.py:126
  364.1 5.8 convolution_convert_fusion.5
  374.2 5.7 convolution_convert_fusion.4
  385.8 318.4 %while.55 = (s32[]{:T(128)}, bf16[256,128]{1,0:T(8,128)(2,1)S(1)}, bf16[2,256,2048]{2,1,0:T(8,128)(2,1)}, pred[]{:T(512)}, s32[]{:T(128)}, /*index=5*/bf16[2,256...) while((s32[]{:T(128)}, bf16[256,128]{1,0:T(8,128)(2,1)S(1)}, ...), condition=%wide.region_8.9_spmd, body=%wide.region_3.8_spmd.sunk | while | flops 677446400 | bytes 32006564 | solution.py:175
  386.6 45.0 %all-gather.18.cloned.1.call-done = bf16[256,2048]{1,0:T(8,128)(2,1)} async-done(((bf16[256,128]{1,0:T(8,128)(2,1)}), bf16[256,2048]{1,0:T(8,128)(2,1)}) %all-gather.18.cloned.1.call-update) | async-done | bytes 1048592 | tf_op jit(solution)/shard_map/while/body/eval_jaxpr/all_gather | solution.py:22
  441.6 44.5 %all-gather.20.cloned.1.call-done = bf16[256,4096]{1,0:T(8,128)(2,1)} async-done(((bf16[256,256]{1,0:T(8,128)(2,1)}), bf16[256,4096]{1,0:T(8,128)(2,1)}) %all-gather.20.cloned.1.call-update) | async-done | bytes 2097168 | tf_op jit(solution)/shard_map/while/body/eval_jaxpr/all_gather | solution.py:22
  492.7 45.0 %all-gather.18.cloned.1.call-done = bf16[256,2048]{1,0:T(8,128)(2,1)} async-done(((bf16[256,128]{1,0:T(8,128)(2,1)}), bf16[256,2048]{1,0:T(8,128)(2,1)}) %all-gather.18.cloned.1.call-update) | async-done | bytes 1048592 | tf_op jit(solution)/shard_map/while/body/eval_jaxpr/all_gather | solution.py:22
  547.6 44.5 %all-gather.20.cloned.1.call-done = bf16[256,4096]{1,0:T(8,128)(2,1)} async-done(((bf16[256,256]{1,0:T(8,128)(2,1)}), bf16[256,4096]{1,0:T(8,128)(2,1)}) %all-gather.20.cloned.1.call-update) | async-done | bytes 2097168 | tf_op jit(solution)/shard_map/while/body/eval_jaxpr/all_gather | solution.py:22
  598.7 45.2 %all-gather.18.cloned.1.call-done = bf16[256,2048]{1,0:T(8,128)(2,1)} async-done(((bf16[256,128]{1,0:T(8,128)(2,1)}), bf16[256,2048]{1,0:T(8,128)(2,1)}) %all-gather.18.cloned.1.call-update) | async-done | bytes 1048592 | tf_op jit(solution)/shard_map/while/body/eval_jaxpr/all_gather | solution.py:22
  653.9 44.5 %all-gather.20.cloned.1.call-done = bf16[256,4096]{1,0:T(8,128)(2,1)} async-done(((bf16[256,256]{1,0:T(8,128)(2,1)}), bf16[256,4096]{1,0:T(8,128)(2,1)}) %all-gather.20.cloned.1.call-update) | async-done | bytes 2097168 | tf_op jit(solution)/shard_map/while/body/eval_jaxpr/all_gather | solution.py:22
  709.1 323.1 %while.56 = (s32[]{:T(128)}, bf16[256,128]{1,0:T(8,128)(2,1)S(1)}, bf16[2,4,512,2,128]{4,3,2,1,0:T(2,128)(2,1)}, bf16[2,4,512,2,128]{4,3,2,1,0:T(2,128)(2,1)}, p...) while((s32[]{:T(128)}, bf16[256,128]{1,0:T(8,128)(2,1)S(1)}, ...), condition=%wide.region_17.18_spmd, body=%wide.region_9.17_spmd.sunk | while | flops 1152261888 | bytes 76540544 | solution.py:216
  715.8 39.3 %all-gather.22.cloned.1.call-done = bf16[256,2048]{1,0:T(8,128)(2,1)} async-done(((bf16[256,128]{1,0:T(8,128)(2,1)}), bf16[256,2048]{1,0:T(8,128)(2,1)}) %all-gather.22.cloned.1.call-update) | async-done | bytes 1048592 | tf_op jit(solution)/shard_map/while/body/eval_jaxpr/all_gather | solution.py:22
  776.5 3.7 fusion.195
  782.7 22.8 %all-gather.3 = bf16[16,1,256]{2,1,0:T(2,128)(2,1)S(1)} all-gather(bf16[1,1,256]{2,1,0:T(2,128)(2,1)S(1)} %reshape.463), channel_id=1, replica_groups=mesh['section'=2,'dp'=4,'mp'=16] {'mp'}, dimensions={0}, use_global_device_ids=true | all-gather | bytes 8704 | tf_op jit(solution)/shard_map/while/body/eval_jaxpr/all_gather | solution.py:28
  823.0 40.1 %all-gather.22.cloned.1.call-done = bf16[256,2048]{1,0:T(8,128)(2,1)} async-done(((bf16[256,128]{1,0:T(8,128)(2,1)}), bf16[256,2048]{1,0:T(8,128)(2,1)}) %all-gather.22.cloned.1.call-update) | async-done | bytes 1048592 | tf_op jit(solution)/shard_map/while/body/eval_jaxpr/all_gather | solution.py:22
  884.5 3.7 fusion.195
  890.7 22.8 %all-gather.3 = bf16[16,1,256]{2,1,0:T(2,128)(2,1)S(1)} all-gather(bf16[1,1,256]{2,1,0:T(2,128)(2,1)S(1)} %reshape.463), channel_id=1, replica_groups=mesh['section'=2,'dp'=4,'mp'=16] {'mp'}, dimensions={0}, use_global_device_ids=true | all-gather | bytes 8704 | tf_op jit(solution)/shard_map/while/body/eval_jaxpr/all_gather | solution.py:28
  931.0 40.1 %all-gather.22.cloned.1.call-done = bf16[256,2048]{1,0:T(8,128)(2,1)} async-done(((bf16[256,128]{1,0:T(8,128)(2,1)}), bf16[256,2048]{1,0:T(8,128)(2,1)}) %all-gather.22.cloned.1.call-update) | async-done | bytes 1048592 | tf_op jit(solution)/shard_map/while/body/eval_jaxpr/all_gather | solution.py:22
  992.5 3.7 fusion.195
  998.6 22.8 %all-gather.3 = bf16[16,1,256]{2,1,0:T(2,128)(2,1)S(1)} all-gather(bf16[1,1,256]{2,1,0:T(2,128)(2,1)S(1)} %reshape.463), channel_id=1, replica_groups=mesh['section'=2,'dp'=4,'mp'=16] {'mp'}, dimensions={0}, use_global_device_ids=true | all-gather | bytes 8704 | tf_op jit(solution)/shard_map/while/body/eval_jaxpr/all_gather | solution.py:28
  1032.2 7.4 fusion.92
  1039.7 6.7 fusion.98
  1046.5 21.9 %all-gather.16.cloned.1.call-done = bf16[3584,256]{1,0:T(8,128)(2,1)} async-done(((bf16[896,256]{1,0:T(8,128)(2,1)}), bf16[3584,256]{1,0:T(8,128)(2,1)}) %all-gather.16.cloned.1.call-update) | async-done | bytes 1835024 | tf_op jit(solution)/shard_map/all_gather | solution.py:233
  1071.1 42.0 %all-reduce.2.cloned.1.call-done = bf16[1,896,256]{2,1,0:T(8,128)(2,1)} async-done(((bf16[1,896,256]{2,1,0:T(8,128)(2,1)}), bf16[1,896,256]{2,1,0:T(8,128)(2,1)}) %all-reduce.2.cloned.1.call-update) | async-done | bytes 458768 | tf_op jit(solution)/shard_map/psum | solution.py:234
  (341 shorter events, 244.2 us)
Async XLA Ops:
  7.2 356.9 %copy-start = (bf16[1,896,256]{2,1,0:T(8,128)(2,1)S(1)}, bf16[1,896,256]{2,1,0:T(8,128)(2,1)}, u32[]{:S(2)}) copy-start(bf16[1,896,256]{2,1,0:T(8,128)(2,1)} %param.36) | copy-start | bytes 1376260
  7.2 2.1 copy-start.9
  7.2 89.1 %all-gather.12.cloned.1.call-start = ((), (), s32[]{:S(2)}) async-start(), calls=%async_computation.2 | async-start | bytes 8912896 | tf_op jit(solution)/shard_map/all_gather | solution.py:22
  9.3 2.9 copy-start.16
  9.3 2.9 copy-start.19
  12.3 84.0 %copy-start.12 = (bf16[4096,56]{0,1:T(8,128)(2,1)S(1)}, bf16[4096,56]{0,1:T(8,128)(2,1)}, u32[]{:S(2)}) copy-start(bf16[4096,56]{0,1:T(8,128)(2,1)} %param.32) | copy-start | bytes 1376260
  16.3 138.2 %all-gather.14.cloned.1.call-start = ((), (), s32[]{:S(2)}) async-start(), calls=%async_computation.3 | async-start | bytes 3784704 | tf_op jit(solution)/shard_map/all_gather | solution.py:116
  103.0 5.1 copy-start.14
  103.0 5.2 copy-start.18
  103.0 5.3 copy-start.15
  103.0 22.6 %all-to-all-start = ((bf16[16,256,128]{2,1,0:T(8,128)(2,1)}), bf16[16,256,128]{2,1,0:T(8,128)(2,1)S(1)}, u32[]{:S(2)}, u32[]{:S(2)}) async-start(bf16[16,256,128]{2,1,0:T(8,128)(2,1)} %bitcast.38), calls=%async_computation | async-start | bytes 2097152 | tf_op jit(solution)/shard_map/all_to_all | solution.py:142
  125.6 20.5 %all-to-all-start.1 = ((bf16[16,128,256]{2,1,0:T(8,128)(2,1)}), bf16[16,128,256]{2,1,0:T(8,128)(2,1)S(1)}, u32[]{:S(2)}, u32[]{:S(2)}) async-start(bf16[16,128,256]{2,1,0:T(8,128)(2,1)} %bitcast.41), calls=%async_computation.1 | async-start | bytes 2097152 | tf_op jit(solution)/shard_map/all_to_all | solution.py:141
  372.4 1.8 copy-start.17
  384.2 1.6 copy-start.10
  384.2 1.6 copy-start.13
  385.8 45.8 %all-gather.18.cloned.1.call-start = ((), (), s32[]{:S(2)}) async-start(), calls=%async_computation.6 | async-start | bytes 1114112 | tf_op jit(solution)/shard_map/while/body/eval_jaxpr/all_gather | solution.py:22
  386.5 99.5 %all-gather.20.cloned.1.call-start = ((), (), s32[]{:S(2)}) async-start(), calls=%async_computation.7 | async-start | bytes 2228224 | tf_op jit(solution)/shard_map/while/body/eval_jaxpr/all_gather | solution.py:22
  438.7 47.4 %copy-start.8 = (bf16[256,128]{1,0:T(8,128)(2,1)S(1)}, bf16[256,128]{1,0:T(8,128)(2,1)}, u32[]{:S(2)}) copy-start(bf16[256,128]{1,0:T(8,128)(2,1)} %bitcast_select_fusion.6) | copy-start | bytes 196612 | tf_op jit(solution)/shard_map/while
  441.6 48.4 %copy-start.2 = (bf16[256,2048]{1,0:T(8,128)(2,1)S(1)}, bf16[256,2048]{1,0:T(8,128)(2,1)}, u32[]{:S(2)}) copy-start(bf16[256,2048]{1,0:T(8,128)(2,1)} %all-gather.18.cloned.1.call-done) | copy-start | bytes 3145732 | tf_op jit(solution)/shard_map/while
  488.6 3.3 collective-permute-start
  491.9 45.7 %all-gather.18.cloned.1.call-start = ((), (), s32[]{:S(2)}) async-start(), calls=%async_computation.6 | async-start | bytes 1114112 | tf_op jit(solution)/shard_map/while/body/eval_jaxpr/all_gather | solution.py:22
  492.6 99.6 %all-gather.20.cloned.1.call-start = ((), (), s32[]{:S(2)}) async-start(), calls=%async_computation.7 | async-start | bytes 2228224 | tf_op jit(solution)/shard_map/while/body/eval_jaxpr/all_gather | solution.py:22
  544.7 47.4 %copy-start.8 = (bf16[256,128]{1,0:T(8,128)(2,1)S(1)}, bf16[256,128]{1,0:T(8,128)(2,1)}, u32[]{:S(2)}) copy-start(bf16[256,128]{1,0:T(8,128)(2,1)} %bitcast_select_fusion.6) | copy-start | bytes 196612 | tf_op jit(solution)/shard_map/while
  547.6 48.4 %copy-start.2 = (bf16[256,2048]{1,0:T(8,128)(2,1)S(1)}, bf16[256,2048]{1,0:T(8,128)(2,1)}, u32[]{:S(2)}) copy-start(bf16[256,2048]{1,0:T(8,128)(2,1)} %all-gather.18.cloned.1.call-done) | copy-start | bytes 3145732 | tf_op jit(solution)/shard_map/while
  594.7 3.2 collective-permute-start
  597.9 46.0 %all-gather.18.cloned.1.call-start = ((), (), s32[]{:S(2)}) async-start(), calls=%async_computation.6 | async-start | bytes 1114112 | tf_op jit(solution)/shard_map/while/body/eval_jaxpr/all_gather | solution.py:22
  598.7 99.8 %all-gather.20.cloned.1.call-start = ((), (), s32[]{:S(2)}) async-start(), calls=%async_computation.7 | async-start | bytes 2228224 | tf_op jit(solution)/shard_map/while/body/eval_jaxpr/all_gather | solution.py:22
  651.1 47.4 %copy-start.8 = (bf16[256,128]{1,0:T(8,128)(2,1)S(1)}, bf16[256,128]{1,0:T(8,128)(2,1)}, u32[]{:S(2)}) copy-start(bf16[256,128]{1,0:T(8,128)(2,1)} %bitcast_select_fusion.6) | copy-start | bytes 196612 | tf_op jit(solution)/shard_map/while
  653.9 48.4 %copy-start.2 = (bf16[256,2048]{1,0:T(8,128)(2,1)S(1)}, bf16[256,2048]{1,0:T(8,128)(2,1)}, u32[]{:S(2)}) copy-start(bf16[256,2048]{1,0:T(8,128)(2,1)} %all-gather.18.cloned.1.call-done) | copy-start | bytes 3145732 | tf_op jit(solution)/shard_map/while
  701.0 3.2 collective-permute-start
  704.3 4.8 copy-start.11
  704.3 4.8 copy-start.20
  709.1 46.0 %all-gather.22.cloned.1.call-start = ((), (), s32[]{:S(2)}) async-start(), calls=%async_computation.8 | async-start | bytes 1114112 | tf_op jit(solution)/shard_map/while/body/eval_jaxpr/all_gather | solution.py:22
  709.8 98.6 %all-gather.24.cloned.1.call-start = ((), (), s32[]{:S(2)}) async-start(), calls=%async_computation.9 | async-start | bytes 2228224 | tf_op jit(solution)/shard_map/while/body/eval_jaxpr/all_gather | solution.py:27
  759.0 2.0 copy-start.21
  765.8 4.7 copy-start.3
  780.2 28.2 %copy-start.7 = (bf16[256,128]{1,0:T(8,128)(2,1)S(1)}, bf16[256,128]{1,0:T(8,128)(2,1)}, u32[]{:S(2)}) copy-start(bf16[256,128]{1,0:T(8,128)(2,1)} %bitcast_select_fusion.7) | copy-start | bytes 196612 | tf_op jit(solution)/shard_map/while
  808.4 4.0 copy-start.4
  811.1 3.8 collective-permute-start.1
  815.0 1.3 copy-start.5
  816.3 46.8 %all-gather.22.cloned.1.call-start = ((), (), s32[]{:S(2)}) async-start(), calls=%async_computation.8 | async-start | bytes 1114112 | tf_op jit(solution)/shard_map/while/body/eval_jaxpr/all_gather | solution.py:22
  817.0 99.4 %all-gather.24.cloned.1.call-start = ((), (), s32[]{:S(2)}) async-start(), calls=%async_computation.9 | async-start | bytes 2228224 | tf_op jit(solution)/shard_map/while/body/eval_jaxpr/all_gather | solution.py:27
  866.9 2.0 copy-start.21
  873.8 4.7 copy-start.3
  888.2 28.2 %copy-start.7 = (bf16[256,128]{1,0:T(8,128)(2,1)S(1)}, bf16[256,128]{1,0:T(8,128)(2,1)}, u32[]{:S(2)}) copy-start(bf16[256,128]{1,0:T(8,128)(2,1)} %bitcast_select_fusion.7) | copy-start | bytes 196612 | tf_op jit(solution)/shard_map/while
  916.4 4.0 copy-start.4
  919.1 3.8 collective-permute-start.1
  922.9 1.3 copy-start.5
  924.2 46.8 %all-gather.22.cloned.1.call-start = ((), (), s32[]{:S(2)}) async-start(), calls=%async_computation.8 | async-start | bytes 1114112 | tf_op jit(solution)/shard_map/while/body/eval_jaxpr/all_gather | solution.py:22
  925.0 99.4 %all-gather.24.cloned.1.call-start = ((), (), s32[]{:S(2)}) async-start(), calls=%async_computation.9 | async-start | bytes 2228224 | tf_op jit(solution)/shard_map/while/body/eval_jaxpr/all_gather | solution.py:27
  974.9 2.0 copy-start.21
  981.8 4.7 copy-start.3
  996.1 28.2 %copy-start.7 = (bf16[256,128]{1,0:T(8,128)(2,1)S(1)}, bf16[256,128]{1,0:T(8,128)(2,1)}, u32[]{:S(2)}) copy-start(bf16[256,128]{1,0:T(8,128)(2,1)} %bitcast_select_fusion.7) | copy-start | bytes 196612 | tf_op jit(solution)/shard_map/while
  1024.4 4.0 copy-start.4
  1027.1 3.8 collective-permute-start.1
  1030.9 1.3 copy-start.5
  1032.2 36.2 %all-gather.16.cloned.1.call-start = ((), (), s32[]{:S(2)}) async-start(), calls=%async_computation.5 | async-start | bytes 2293760 | tf_op jit(solution)/shard_map/all_gather | solution.py:233
  1032.2 7.5 copy-start.6
  1039.6 73.5 %all-reduce.2.cloned.1.call-start = ((), (), s32[]{:S(2)}) async-start(), calls=%async_computation.4 | async-start | bytes 917504 | tf_op jit(solution)/shard_map/psum | solution.py:234
  1039.7 75.2 %copy-start.1 = (bf16[1,896,256]{2,1,0:T(8,128)(2,1)S(1)}, bf16[1,896,256]{2,1,0:T(8,128)(2,1)}, u32[]{:S(2)}) copy-start(bf16[1,896,256]{2,1,0:T(8,128)(2,1)} %param.36) | copy-start | bytes 1376260
Sparse Core Ops, SparseCore 0:
  16.4 79.8 all-gather.11
  103.2 51.2 all-gather.13
  389.3 42.2 all-gather.17
  439.7 46.3 all-gather.19
  495.1 42.5 all-gather.17
  545.7 46.3 all-gather.19
  601.4 42.5 all-gather.17
  652.0 46.3 all-gather.19
  712.6 42.5 all-gather.21
  762.0 46.4 all-gather.23
  819.7 43.2 all-gather.21
  869.9 46.3 all-gather.23
  927.7 43.2 all-gather.21
  977.9 46.4 all-gather.23
  1039.8 28.5 all-gather.15
  1070.6 42.4 all-reduce.1
